TPU v7x, 32 devices: a whole 2x2x4 slice. The times are simulated.
32 devices in a mesh: band: 8 (over z, x), lon: 4 (over y, core).
Axes of the slice: x: 2, y: 2, z: 4, core: 2. Of those that a mesh axis runs over, the one named last changes fastest.
Arguments:
- loads: float32 [2, 2, 32, 4096], P(None, None, 'band', 'lon'), may hold values from -6 to 6
- legendre: bfloat16 [1024, 1024, 32], P('band', 'lon'), may hold values from -1 to 1
- love: float32 [2, 2, 1024], P(None, None, 'lon'), may hold values from -4 to 4
- cycle_weight: float32 [32], replicated, may hold values from 0.25 to 1
- order_list: int32 [1024], replicated, may hold values from 0 to 1023, as said below
- cycle_order: int32 [32], replicated, may hold values from 0 to 31, each once
Outputs:
- sea_response: float32 [2, 2, 32, 4096], P(None, None, 'band', 'lon')
Inputs may be any that keep to these rules, and one draw needn't show every extreme that they name: `order_list`: entries b * 128 to b * 128 + 127 are the orders held by band index b; every order appears once, and the orders of every band index have the same sum. Row j of the grid holds cycle pair cycle_order[j].
All inputs are finite; a program needn't handle non-finite values.
Results may differ from a plain program's by a relative error of at most 0.0041.
Values may be sent and summed in bfloat16 or wider, within the bound.
No kernel may reach another device: no remote copies, remote signals or barrier semaphores. Data moves between devices by JAX's collectives and lax.ppermute only.
A program may use at most 64 MiB of HBM per device.

v0:
```python
import functools
import math

import jax
import jax.numpy as jnp
from jax import lax
from jax.experimental import pallas as pl
from jax.experimental.pallas import tpu as pltpu
from jax.sharding import PartitionSpec as P


LANES = 128
ROWS = 8
VMEM_LIMIT = 12 << 20
NT = (((1,), (1,)), ((), ()))


def iota(shape, axis):
    return lax.broadcasted_iota(jnp.int32, shape, axis)


def turn(phase, total):
    shift = (total // 4).bit_length() - 1
    quadrant = (phase + total // 8) >> shift
    x = (phase - (quadrant << shift)).astype(jnp.float32) * (2.0 * math.pi / total)
    z = x * x
    s = ((-1.9515295891e-4 * z + 8.3321608736e-3) * z - 1.6666654611e-1) * z * x + x
    c = ((2.443315711809948e-5 * z - 1.388731625493765e-3) * z + 4.166664568298827e-2) * z * z
    c = c - 0.5 * z + 1.0
    odd = (quadrant & 1) == 1
    cosine = jnp.where(odd, s, c)
    sine = jnp.where(odd, c, s)
    cosine = jnp.where(((quadrant + 1) & 2) == 2, -cosine, cosine)
    sine = jnp.where((quadrant & 2) == 2, -sine, sine)
    return cosine, sine


def split(x):
    high = x.astype(jnp.bfloat16)
    return high, (x - high.astype(jnp.float32)).astype(jnp.bfloat16)


def dot(a, b):
    return jnp.dot(a, b, preferred_element_type=jnp.float32)


def dot_nt(a, b):
    return lax.dot_general(a, b, NT, preferred_element_type=jnp.float32)


def analyse_grid(total, after_ref, right_ref, turn_ref, weight_ref, cycle_ref, *refs):
    del after_ref
    parts, out_ref, points_ref, mid_ref = refs[:-3], refs[-3], refs[-2], refs[-1]
    cycles = parts[0].shape[2]
    blocks = parts[0].shape[3] // LANES
    count, width = turn_ref.shape[1:]
    owners = width // (LANES // 2)
    lon_count = out_ref.shape[0] // owners
    quarter = width // owners // 2
    pieces = LANES // quarter
    step = 2 * cycles

    for q, part in enumerate(parts):
        for a in range(blocks):
            for f in range(2):
                north = part[f, 0, :, a * LANES : (a + 1) * LANES]
                south = part[f, 1, :, a * LANES : (a + 1) * LANES]
                at = ((q * blocks + a) * 2 + f) * step
                points_ref[at : at + step] = jnp.concatenate([north + south, north - south], axis=0)
    high, low = split(points_ref[...])
    mid_ref[...] = dot(jnp.concatenate([high, low, high], axis=1), right_ref[...])

    sums = [[jnp.zeros((step, width), jnp.float32) for _ in range(2)] for _ in range(2)]
    for a in range(count):
        ca, sa = turn_ref[0, a : a + 1], turn_ref[1, a : a + 1]
        for f in range(2):
            at = (a * 2 + f) * step
            tc = mid_ref[at : at + step, :width]
            ts = mid_ref[at : at + step, width:]
            sums[f][0] = sums[f][0] + (ca * tc - sa * ts)
            sums[f][1] = sums[f][1] - (sa * tc + ca * ts)

    slot = iota((1, LANES), 1) // quarter
    northern = cycle_ref.shape[1]
    lane = iota((step, northern), 1)
    row = lax.axis_index("band") * cycles + iota((step, northern), 0) % cycles
    listed = jnp.sum(jnp.where(lane == row, cycle_ref[...].astype(jnp.float32), 0.0), axis=1, keepdims=True)
    weight = jnp.sum(jnp.where(lane == listed.astype(jnp.int32), weight_ref[...], 0.0), axis=1, keepdims=True)
    weight = weight * (1.0 / math.sqrt(total))
    for owner in range(owners):
        for side in range(2):
            t, i = (2 * owner + side) // pieces, (2 * owner + side) % pieces
            block = None
            for e in range(4):
                piece = sums[e // 2][e % 2][:, t * LANES : (t + 1) * LANES]
                move = (e - i) * quarter % LANES
                piece = pltpu.roll(piece, move, 1) if move else piece
                block = piece if block is None else jnp.where(slot == e, piece, block)
            block = block * weight
            for q in range(side, lon_count, 2):
                out_ref[owner * lon_count + q] = block


def add_points(parts_ref, out_ref):
    sides, owners = out_ref.shape[:2]
    lon_count = parts_ref.shape[0] // owners
    for c in range(sides):
        for b in range(owners):
            value = parts_ref[b * lon_count + c]
            for q in range(c + sides, lon_count, sides):
                value = value + parts_ref[b * lon_count + q]
            out_ref[c, b] = value.astype(out_ref.dtype)


def products(fine, coarse):
    for k in range(coarse[0].shape[0]):
        cc, cs = coarse[0][k : k + 1], coarse[1][k : k + 1]
        yield fine[0] * cc - fine[1] * cs, fine[1] * cc + fine[0] * cs


def opening(out_ref):
    out_ref[...] = jnp.zeros_like(out_ref)


def forward_tables(blocks, total, orders_ref, after_ref, right_ref, first_ref):
    del after_ref
    owners, per_owner = orders_ref.shape
    share = per_owner // 2
    lon = lax.axis_index("lon")
    side = lon % 2
    first_lanes = iota((1, LANES), 1) < share

    mine = pltpu.roll(orders_ref[...], (LANES - share * side) % LANES, 1)
    moved = pltpu.roll(mine, share, 1)
    orders = jnp.concatenate(
        [jnp.where(first_lanes, mine[b : b + 1], moved[b + 1 : b + 2]) for b in range(0, owners, 2)], axis=1
    )
    width = orders.shape[1]
    fine = turn(iota((ROWS, width), 0) * orders, total)
    coarse = turn((iota((LANES // ROWS, width), 0) * ROWS * orders) & (total - 1), total)
    kept = []
    for k, pair in enumerate(products(fine, coarse)):
        kept.append([split(table) for table in pair])
        if k % 2 == 0:
            continue
        for c in range(2):
            high, low = [jnp.concatenate([kept[k - 1][c][i], kept[k][c][i]], axis=0) for i in range(2)]
            for i, value in enumerate((high, high, low)):
                at = i * LANES + (k - 1) * ROWS
                right_ref[at : at + 2 * ROWS, c * width : (c + 1) * width] = value
    for k in range(2):
        origin = lon if k == 0 else lon + 1 - 2 * side
        step = iota((blocks, width), 0) + origin * blocks
        for c, table in enumerate(turn((step * LANES * orders) & (total - 1), total)):
            first_ref[c, k * blocks : (k + 1) * blocks] = table


def cycle_tables(owners, cycles, after_ref, cycle_ref, pick_ref, put_ref):
    del after_ref
    northern = owners * cycles
    lane = iota((1, LANES), 1)

    listed = jnp.broadcast_to(cycle_ref[...].astype(jnp.float32), (LANES, northern)).astype(jnp.bfloat16)
    index = iota((LANES, northern), 0)

    def places(repeat):
        place = index // (repeat * cycles) * cycles + index % cycles
        return jnp.where(place == iota((LANES, northern), 1), 1.0, 0.0).astype(jnp.bfloat16)

    arriving = dot_nt(listed[: 2 * ROWS], places(2))[:1].astype(jnp.int32)
    found = (iota((northern, LANES), 0) == arriving) & (lane < 2 * northern)
    for p in range(2):
        one = jnp.where(found & (lane // cycles % 2 == p), 1.0, 0.0)
        copies = jnp.concatenate([one] * (LANES // northern), axis=0)
        pick_ref[p * LANES : (p + 1) * LANES] = copies.astype(jnp.bfloat16)
    leaving = dot_nt(places(4), listed).astype(jnp.int32)
    found = leaving == iota((LANES, LANES), 1) % northern
    part = iota((LANES, LANES), 0) // cycles % 4
    for i in range(4):
        put = jnp.where(found & (part == i), 1.0, 0.0)
        put_ref[i // 2, :, i % 2 * LANES : (i % 2 + 1) * LANES] = put.astype(jnp.bfloat16)


def inverse_tables(total, orders_ref, after_ref, rows_ref, turn_ref, basis_ref):
    del after_ref
    owners, per_owner = orders_ref.shape
    blocks = turn_ref.shape[2]
    quarter = per_owner // 4
    lon = lax.axis_index("lon")
    own = orders_ref[pl.ds(lax.axis_index("band"), 1), :].astype(jnp.float32)
    rows_ref[...] = jnp.transpose(jnp.broadcast_to(own, (LANES, per_owner))).astype(jnp.int32)

    slot = iota((1, LANES), 1) // quarter
    orders = orders_ref[...]
    ahead, behind = pltpu.roll(orders, LANES - quarter, 1), pltpu.roll(orders, quarter, 1)
    arranged = jnp.where(slot == 1, ahead, jnp.where(slot == 2, behind, orders))
    scale = 1.0 / math.sqrt(total)
    for b in range(owners):
        order = arranged[b : b + 1]
        factor = jnp.where(order == 0, scale, 2.0 * scale)
        step = iota((blocks, per_owner), 0) + lon * blocks
        for c, table in enumerate(turn((step * LANES * order) & (total - 1), total)):
            turn_ref[c, b] = table * factor
        fine = turn(iota((ROWS, per_owner), 0) * order, total)
        coarse = turn((iota((LANES // ROWS, per_owner), 0) * ROWS * order) & (total - 1), total)
        kept = []
        for k, pair in enumerate(products(fine, coarse)):
            kept.append(pair)
            if k % 2 == 1:
                rows = slice((k - 1) * ROWS, (k + 1) * ROWS)
                for c in range(2):
                    at = (c * owners + b) * per_owner
                    both = jnp.concatenate([kept[k - 1][c], kept[k][c]], axis=0)
                    basis_ref[rows, at : at + per_owner] = both.astype(basis_ref.dtype)


def spectral(
    pick_ref,
    put_ref,
    rows_ref,
    folded_ref,
    own_table_ref,
    other_table_ref,
    own_love_ref,
    other_love_ref,
    out_ref,
    spread_ref,
    kept_ref,
):
    parts, owners, height = folded_ref.shape[:3]
    quarter = rows_ref.shape[0] // (2 * parts)
    degrees = own_table_ref.shape[1]
    northern = owners * height // 2
    group = degrees // northern
    wide = group * northern
    lon = lax.axis_index("lon")
    side = lon % 2

    pad = jnp.zeros((LANES - 2 * northern, LANES), jnp.float32)
    turned = []
    for q in range(parts):
        pieces = [folded_ref[q, b].astype(jnp.float32) for b in range(owners)]
        turned.append(jnp.transpose(jnp.concatenate(pieces + [pad], axis=0)))
    spread_ref[...] = dot_nt(jnp.concatenate(turned, axis=0).astype(jnp.bfloat16), pick_ref[...])

    lane = iota((ROWS, degrees), 1)
    degree = [lon * degrees + lane, (lon + 1 - 2 * side) * degrees + lane]
    tables = [own_table_ref, other_table_ref]
    love = [[[ref[g, f : f + 1, :] for f in range(2)] for g in range(2)] for ref in (own_love_ref, other_love_ref)]
    diagonal = iota((ROWS, wide), 0) == iota((ROWS, wide), 1) // northern
    across = LANES // northern
    upper = iota((ROWS, LANES), 0) < across
    folded_diagonal = iota((ROWS, LANES), 0) % across == iota((ROWS, LANES), 1) // northern
    groups = parts * quarter // group

    def first_order(n):
        q, first = n * group // quarter, n * group % quarter
        return (2 * q + side) * quarter + first

    def table(n, d):
        return tables[d][pl.ds(pl.multiple_of(first_order(n) * northern, wide), wide)]

    def spread(n):
        q, first = n * group // quarter, n * group % quarter
        left = []
        for f in range(2):
            for p in range(2):
                for c in range(2):
                    at = q * LANES + (f * 2 + c) * quarter + first
                    piece = spread_ref[at : at + group, p * LANES : (p + 1) * LANES]
                    left.append(jnp.where(diagonal, jnp.concatenate([piece] * (wide // LANES), axis=1), 0.0))
        return jnp.concatenate(left, axis=0).astype(jnp.bfloat16)

    def respond(n, d, analysed):
        order = rows_ref[pl.ds(pl.multiple_of(first_order(n), group), group)]
        gap = degree[d] - jnp.concatenate([order] * (degrees // LANES), axis=1)
        valid = gap >= 0
        keep = [valid & ((gap & 1) == p) for p in range(2)]
        mixed = []
        for g in range(2):
            for p in range(2):
                for c in range(2):
                    lo = (p * 2 + c) * group
                    hi = ((2 + p) * 2 + c) * group
                    value = love[d][g][0] * analysed[lo : lo + group] + love[d][g][1] * analysed[hi : hi + group]
                    mixed.append(jnp.where(keep[p], value, 0.0))
        return dot_nt(jnp.concatenate(mixed, axis=0).astype(jnp.bfloat16), table(n, d))

    def keep_pair(n, halves):
        for g in range(2):
            for c in range(2):
                lo, hi = (g * 4 + c) * group, (g * 4 + 2 + c) * group
                at = c * parts * quarter + n * group
                rows = []
                for half in halves:
                    even, odd = half[lo : lo + group], half[hi : hi + group]
                    even = jnp.where(upper, even[:, :LANES], even[:, LANES:])
                    odd = jnp.where(upper, odd[:, :LANES], odd[:, LANES:])
                    rows.append([jnp.where(folded_diagonal, x, 0.0) for x in (even + odd, even - odd)])
                for h in range(2):
                    both = jnp.concatenate([row[h] for row in rows], axis=0).astype(jnp.bfloat16)
                    kept_ref[g, at : at + 2 * group, h * LANES : (h + 1) * LANES] = both

    steps = [(n, d) for n in range(groups) for d in range(2)]
    left, analysed, partial = None, {}, {}
    for i in range(len(steps) + 2):
        if i < len(steps):
            n, d = steps[i]
            left = spread(n) if d == 0 else left
            analysed[i] = dot(left, table(n, d))
        if 1 <= i <= len(steps):
            n, d = steps[i - 1]
            value = respond(n, d, analysed.pop(i - 1))
            partial[n] = value if d == 0 else partial[n] + value
        if i >= 5 and i % 4 == 1:
            n = (i - 5) // 2
            keep_pair(n, [partial.pop(n), partial.pop(n + 1)])

    total = dot_nt(put_ref[0], kept_ref[0]) + dot_nt(put_ref[1], kept_ref[1])
    total = total.astype(out_ref.dtype)
    lon_count = out_ref.shape[0] // owners
    rows = out_ref.shape[1]
    for b in range(owners):
        for q in range(lon_count):
            out_ref[b * lon_count + q] = total[b * rows : (b + 1) * rows]


def synthesise_grid(turn_ref, basis_ref, values_ref, out_ref, left_ref):
    owners, blocks, per_owner = turn_ref.shape[1:]
    lon_count = values_ref.shape[0] // owners
    rows = values_ref.shape[1]
    cycles = out_ref.shape[2]
    count = owners * per_owner
    height = blocks * rows
    first_lanes = iota((1, LANES), 1) < per_owner // 2
    for b in range(owners):
        halves = []
        for c in range(2):
            value = values_ref[b * lon_count + c].astype(jnp.float32)
            for q in range(c + 2, lon_count, 2):
                value = value + values_ref[b * lon_count + q].astype(jnp.float32)
            halves.append(value)
        re = jnp.where(first_lanes, halves[0], pltpu.roll(halves[1], per_owner // 2, 1))
        im = jnp.where(first_lanes, pltpu.roll(halves[0], per_owner // 2, 1), halves[1])
        at = b * per_owner
        for a in range(blocks):
            ca, sa = turn_ref[0, b, a : a + 1], turn_ref[1, b, a : a + 1]
            for c, term in ((0, ca * re - sa * im), (1, -(sa * re + ca * im))):
                high, low = split(term)
                lanes = slice(c * count + at, c * count + at + per_owner)
                left_ref[a * rows : (a + 1) * rows, lanes] = high
                left_ref[height + a * rows : height + (a + 1) * rows, lanes] = low
    grid = dot_nt(left_ref[...], basis_ref[...])
    grid = grid[:height] + grid[height:]
    for a in range(blocks):
        for g in range(2):
            for h in range(2):
                at = a * rows + (g * 2 + h) * cycles
                out_ref[g, h, :, a * LANES : (a + 1) * LANES] = grid[at : at + cycles]


def fits(owners, lon_count, cycles, points, per_owner, degrees):
    northern = owners * cycles
    total = points * lon_count
    return (
        per_owner == LANES
        and 4 * per_owner == lon_count * LANES
        and lon_count % 2 == 0
        and 2 * cycles == ROWS
        and 4 * northern == LANES
        and ROWS * northern == degrees
        and degrees % LANES == 0
        and owners == ROWS
        and points % LANES == 0
        and total & (total - 1) == 0
        and owners * per_owner * LANES < 1 << 24
    )


def per_device_kernels(loads, legendre, love, cycle_weight, order_list, cycle_order):
    owners = lax.axis_size("band")
    lon_count = lax.axis_size("lon")
    cycles, points = loads.shape[2], loads.shape[3]
    per_owner, degrees, northern = legendre.shape
    total = points * lon_count
    devices = owners * lon_count
    blocks = points // LANES
    everyone = ("band", "lon")
    vmem = pl.BlockSpec(memory_space=pltpu.VMEM)
    table = order_list.reshape(owners, per_owner)
    cycle_list = cycle_order.reshape(1, northern)

    def kernel(body, out_shape, in_specs, scratch_shapes, flops):
        return pl.pallas_call(
            body,
            out_shape=out_shape,
            in_specs=in_specs,
            out_specs=jax.tree.map(lambda _: vmem, out_shape),
            scratch_shapes=scratch_shapes,
            compiler_params=pltpu.CompilerParams(vmem_limit_bytes=VMEM_LIMIT),
            cost_estimate=pl.CostEstimate(flops=flops, bytes_accessed=1 << 20, transcendentals=0),
        )

    partner = [(i, i ^ 1) for i in range(lon_count)]
    rows = jnp.transpose(legendre, (0, 2, 1)).reshape(per_owner * northern, degrees)
    parts = [loads, lax.ppermute(loads, "lon", partner)]
    other_rows = lax.ppermute(rows, "lon", partner)
    other_love = lax.ppermute(love, "lon", partner)
    count = 2 * blocks
    width = owners * per_owner // 2
    opened = kernel(opening, jax.ShapeDtypeStruct((ROWS, LANES), jnp.float32), [], [], 1 << 34)()
    right, first = kernel(
        functools.partial(forward_tables, blocks, total),
        (
            jax.ShapeDtypeStruct((3 * LANES, 2 * width), jnp.bfloat16),
            jax.ShapeDtypeStruct((2, count, width), jnp.float32),
        ),
        [vmem, vmem],
        [],
        1 << 34,
    )(table, opened)
    order_rows, turns, basis = kernel(
        functools.partial(inverse_tables, total),
        (
            jax.ShapeDtypeStruct((per_owner, LANES), jnp.int32),
            jax.ShapeDtypeStruct((2, owners, blocks, per_owner), jnp.float32),
            jax.ShapeDtypeStruct((LANES, 2 * owners * per_owner), jnp.bfloat16),
        ),
        [vmem, vmem],
        [],
        1 << 20,
    )(table, first)
    pick, put = kernel(
        functools.partial(cycle_tables, owners, cycles),
        (
            jax.ShapeDtypeStruct((2 * LANES, LANES), jnp.bfloat16),
            jax.ShapeDtypeStruct((2, LANES, 2 * LANES), jnp.bfloat16),
        ),
        [vmem, vmem],
        [],
        1 << 20,
    )(order_rows, cycle_list)
    sums = kernel(
        functools.partial(analyse_grid, total),
        jax.ShapeDtypeStruct((devices, 2 * cycles, LANES), jnp.float32),
        [vmem] * (5 + len(parts)),
        [
            pltpu.VMEM((count * 4 * cycles, LANES), jnp.float32),
            pltpu.VMEM((count * 4 * cycles, 2 * width), jnp.float32),
        ],
        1 << 24,
    )(pick, right, first, cycle_weight.reshape(1, northern), cycle_list, *parts)
    arrived = lax.all_to_all(sums, everyone, split_axis=0, concat_axis=0, tiled=True)
    folded = kernel(
        add_points,
        jax.ShapeDtypeStruct((2, owners, 2 * cycles, LANES), jnp.bfloat16),
        [vmem],
        [],
        1 << 28,
    )(arrived)
    values = kernel(
        spectral,
        jax.ShapeDtypeStruct((devices, 4 * cycles, per_owner), jnp.bfloat16),
        [vmem] * 8,
        [
            pltpu.VMEM((2 * LANES, 2 * LANES), jnp.float32),
            pltpu.VMEM((2, per_owner, 2 * LANES), jnp.bfloat16),
        ],
        1 << 31,
    )(pick, put, order_rows, folded, rows, other_rows, love, other_love)
    returned = lax.all_to_all(values, everyone, split_axis=0, concat_axis=0, tiled=True)

    return kernel(
        synthesise_grid,
        jax.ShapeDtypeStruct(loads.shape, jnp.float32),
        [vmem] * 3,
        [pltpu.VMEM((2 * 4 * cycles * blocks, 2 * owners * per_owner), jnp.bfloat16)],
        1 << 31,
    )(turns, basis, returned)


def per_device(loads, legendre, love, cycle_weight, order_list, cycle_order):
    sizes = (lax.axis_size("band"), lax.axis_size("lon"), loads.shape[2], loads.shape[3], legendre.shape[0], legendre.shape[1])
    form = per_device_kernels if fits(*sizes) else per_device_plain
    return form(loads, legendre, love, cycle_weight, order_list, cycle_order)


def cycle_basis(order_ids, positions, total):
    phase = positions[:, None] * order_ids[None, :] % total
    angle = phase.astype(jnp.float32) * (2.0 * math.pi / total)
    scale = 1.0 / math.sqrt(total)
    return (jnp.cos(angle) * scale, jnp.sin(angle) * scale)


def per_device_plain(loads, legendre, love, cycle_weight, order_list, cycle_order):
    highest = lax.Precision.HIGHEST
    owners = lax.axis_size("band")
    lon_count = lax.axis_size("lon")
    band_index = lax.axis_index("band")
    lon_index = lax.axis_index("lon")
    cycle_pairs = loads.shape[2]
    points = loads.shape[3]
    total = points * lon_count
    orders = order_list.shape[0]
    per_owner = legendre.shape[0]
    degree_count = legendre.shape[1]
    northern = legendre.shape[2]
    quarter = per_owner // lon_count
    positions = lon_index * points + jnp.arange(points, dtype=jnp.int32)
    cosine, sine = cycle_basis(order_list, positions, total)
    my_cycles = lax.dynamic_slice_in_dim(cycle_order, band_index * cycle_pairs, cycle_pairs)
    picker = my_cycles[:, None] == jnp.arange(northern, dtype=jnp.int32)[None, :]
    weights = jnp.sum(jnp.where(picker, cycle_weight[None, :], 0.0), axis=1)
    forward = jnp.stack([cosine, -sine], axis=1)
    spectrum = jnp.einsum("fhjx,xrm->fhjrm", loads, forward, precision=highest)
    spectrum = spectrum.reshape(2, 2, cycle_pairs, 2, owners, per_owner)
    summed = lax.psum_scatter(spectrum, "lon", scatter_dimension=5, tiled=True)
    cycle_scale = weights[None, :, None, None, None]
    symmetric = ((summed[:, 0] + summed[:, 1]) * cycle_scale).astype(jnp.bfloat16)
    antisym = ((summed[:, 0] - summed[:, 1]) * cycle_scale).astype(jnp.bfloat16)
    folded = jnp.stack([symmetric, antisym], axis=1)
    slot_width = folded.shape[5]
    outgoing = jnp.transpose(folded, (4, 5, 0, 1, 3, 2)).reshape(owners, slot_width, 8, cycle_pairs)
    arrived = lax.all_to_all(outgoing, "band", split_axis=0, concat_axis=3, tiled=True).reshape(
        slot_width, 8, northern
    )
    columns = lax.all_gather(arrived, "lon", axis=0, tiled=True)
    inverse_rows = jnp.argsort(cycle_order)
    columns_sorted = jnp.take(columns, inverse_rows, axis=2)
    my_orders = lax.dynamic_slice_in_dim(order_list, band_index * per_owner, per_owner)
    degrees = lon_index * degree_count + jnp.arange(degree_count, dtype=jnp.int32)
    analysed = jnp.einsum(
        "olk,ock->ocl", legendre, columns_sorted, preferred_element_type=jnp.float32
    )
    analysed = analysed.reshape(per_owner, 2, 2, 2, degree_count)
    even = (degrees[None, :] - my_orders[:, None]) % 2 == 0
    valid = degrees[None, :] >= my_orders[:, None]
    selected = jnp.where(even[:, None, None, :], analysed[:, :, 0], analysed[:, :, 1])
    selected = selected * valid[:, None, None, :].astype(jnp.float32)
    response = jnp.einsum("gfl,ofrl->ogrl", love, selected, precision=highest).astype(jnp.bfloat16)
    even_part = jnp.where((even & valid)[:, None, None, :], response, jnp.zeros_like(response))
    odd_part = jnp.where((~even & valid)[:, None, None, :], response, jnp.zeros_like(response))
    stacked = jnp.stack([even_part, odd_part], axis=2).reshape(per_owner, 8, degree_count)
    partial_sorted = jnp.einsum(
        "olk,ocl->ock", legendre, stacked, preferred_element_type=jnp.float32
    )
    partial_value = jnp.take(partial_sorted, cycle_order, axis=2)
    reduced = lax.psum_scatter(partial_value, "lon", scatter_dimension=0, tiled=True)
    returned = lax.all_to_all(reduced, "band", split_axis=2, concat_axis=0, tiled=True)
    gathered = lax.all_gather(returned[None], "lon", axis=0, tiled=True).reshape(
        orders, 8, cycle_pairs
    )
    slot_ids = jnp.transpose(order_list.reshape(owners, lon_count, quarter), (1, 0, 2)).reshape(
        orders
    )
    cosine_back, sine_back = cycle_basis(slot_ids, positions, total)
    pieces = gathered.reshape(orders, 2, 2, 2, cycle_pairs)
    cycle_values = jnp.stack(
        [pieces[:, :, 0] + pieces[:, :, 1], pieces[:, :, 0] - pieces[:, :, 1]], axis=2
    )
    factor = jnp.where(slot_ids == 0, 1.0, 2.0).astype(jnp.float32)
    inverse = jnp.stack([cosine_back.T, -sine_back.T], axis=0)
    scaled = cycle_values * factor[:, None, None, None, None]
    return jnp.einsum("sghrp,rsx->ghpx", scaled, inverse, precision=highest)


def solution(mesh):
    return jax.shard_map(
        per_device,
        mesh=mesh,
        in_specs=(
            P(None, None, "band", "lon"),
            P("band", "lon", None),
            P(None, None, "lon"),
            P(),
            P(),
            P(),
        ),
        out_specs=P(None, None, "band", "lon"),
        check_vma=False,
    )
```

profile of v0, /device:TPU:0, one launch (start us, length us, event | category | flops | bytes accessed | tf_op | source)
XLA Modules:
  0.0 33.3 jit_solution(17228612034253291356)
XLA Ops:
  0.0 0.5 %collective-permute-start = (f32[2,2,4,1024]{3,2,1,0:T(4,128)}, f32[2,2,4,1024]{3,2,1,0:T(4,128)S(1)}, u32[]{:S(2)}, u32[]{:S(2)}) collective-permute-start(f32[2,2,4,1024]{3,2,1,0:T(4,128)} %refs_0_.1), channel_id=1, source_target_pairs={{0,1},{1,0},{2,3},{3,2},{4,5},{5,4},{6,7},{7,6},{8,9},{9,8},{10,11... | collective-permute-start | bytes 196616 | tf_op jit(solution)/shard_map/ppermute | solution.py:406
  0.5 0.0 copy-start.1
  0.5 0.1 collective-permute-start.1
  0.6 0.6 %copy-done.1 = s32[1024]{0:T(1024)S(1)} copy-done((s32[1024]{0:T(1024)S(1)}, s32[1024]{0:T(1024)}, u32[]{:S(2)}) %copy-start.1) | copy-done | bytes 4120
  1.2 0.0 copy-start.2
  1.2 0.0 copy-start
  1.2 0.0 copy-start.3
  1.2 0.0 copy-start.5
  1.2 0.5 %shard_map.65 = (bf16[384,1024]{1,0:T(8,128)(2,1)S(1)}, f32[2,16,512]{2,1,0:T(8,128)S(1)}) custom-call(s32[8,128]{1,0:T(8,128)S(1)} %bitcast.6, f32[8,128]{1,0:T(8,128)S(1)} %shard_map.64.after_ref), custom_call_target="tpu_custom_call" | custom-call | flops 17179869184 | bytes 1048576 | tf_op jit(solution)/shard_map/pallas_call | solution.py:412
  1.6 0.0 copy-start.4
  1.7 0.4 %shard_map.66 = (s32[128,128]{1,0:T(8,128)S(1)}, f32[2,8,8,128]{3,2,1,0:T(8,128)S(1)}, bf16[128,2048]{1,0:T(8,128)(2,1)S(1)}) custom-call(s32[8,128]{1,0:T(8,128)S(1)} %bitcast.7, f32[2,16,512]{2,1,0:T(8,128)S(1)} %get-tuple-element.12.after_ref.turn_ref), custom_call_target="tpu_custom_call" | custom-call | flops 1048576 | bytes 1048576 | tf_op jit(solution)/shard_map/pallas_call | solution.py:422
  2.1 0.0 copy-done.2
  2.1 0.2 shard_map.67
  2.3 0.0 collective-permute-done.refs_1_
  2.3 0.0 copy-done
  2.3 0.0 copy-done.3
  2.3 1.3 %shard_map.68 = f32[32,8,128]{2,1,0:T(8,128)} custom-call(bf16[256,128]{1,0:T(8,128)(2,1)S(1)} %get-tuple-element.16.after_ref.pick_ref, bf16[384,1024]{1,0:T(8,128)(2,1)S(1)} %get-tuple-element.18.right_ref, f32[2,16,512]{2,1,0:T(8,128)S(1)} %get-tuple-element.12.after_ref.turn_ref, f32[1,32]{1,0:T(1,128)S(1)} %bitcast.10, s32[1,32]{1,0:T(1,128)S(1)} %bitcast.9, ...), custom_call_target="tpu_custom_call" | custom-call | flops 16777216 | bytes 1048576 | tf_op jit(solution)/shard_map/pallas_call | solution.py:443
  3.6 6.9 %all-to-all-start = ((f32[32,8,128]{2,1,0:T(8,128)}), f32[32,8,128]{2,1,0:T(8,128)S(1)}, u32[]{:S(2)}, u32[]{:S(2)}) async-start(f32[32,8,128]{2,1,0:T(8,128)} %shard_map.68), calls=%async_computation | async-start | bytes 262144 | tf_op jit(solution)/shard_map/all_to_all | solution.py:453
  10.6 0.0 copy-done.5
  10.6 0.3 collective-permute-start.2
  10.9 7.9 %all-to-all-done.parts_ref = f32[32,8,128]{2,1,0:T(8,128)S(1)} async-done(((f32[32,8,128]{2,1,0:T(8,128)}), f32[32,8,128]{2,1,0:T(8,128)S(1)}, u32[]{:S(2)}, u32[]{:S(2)}) %all-to-all-start) | async-done | bytes 131104 | tf_op jit(solution)/shard_map/all_to_all | solution.py:453
  18.8 0.0 collective-permute-done.2.other_love_ref
  18.8 0.0 collective-permute-done.1.other_table_ref
  18.8 0.0 copy-done.4
  18.8 3.2 %shard_map.70 = bf16[32,16,128]{2,1,0:T(8,128)(2,1)S(1)} custom-call(bf16[256,128]{1,0:T(8,128)(2,1)S(1)} %get-tuple-element.16.after_ref.pick_ref, bf16[2,128,256]{2,1,0:T(8,128)(2,1)S(1)} %get-tuple-element.17.put_ref, s32[128,128]{1,0:T(8,128)S(1)} %get-tuple-element.15.after_ref.rows_ref, bf16[2,8,8,128]{3,2,1,0:T(8,128)(2,1)S(1)} %shard_map.69.folded_ref, ...), custom_call_target="tpu_custom_call" | custom-call | flops 2147483648 | bytes 1048576 | tf_op jit(solution)/shard_map/pallas_call | solution.py:461
  22.0 10.0 %all_to_all.10.values_ref = bf16[32,16,128]{2,1,0:T(8,128)(2,1)S(1)} all-to-all(bf16[32,16,128]{2,1,0:T(8,128)(2,1)S(1)} %shard_map.70), channel_id=1, replica_groups=mesh['band'=8,'lon'=4] {'band','lon'}, dimensions={0} | all-to-all | bytes 262144 | tf_op jit(solution)/shard_map/all_to_all | solution.py:471
  32.0 1.3 %shard_map.71 = f32[2,2,4,1024]{3,2,1,0:T(4,128)} custom-call(f32[2,8,8,128]{3,2,1,0:T(8,128)S(1)} %get-tuple-element.13.turn_ref, bf16[128,2048]{1,0:T(8,128)(2,1)S(1)} %get-tuple-element.14.basis_ref, bf16[32,16,128]{2,1,0:T(8,128)(2,1)S(1)} %all_to_all.10.values_ref), custom_call_target="tpu_custom_call" | custom-call | flops 2147483648 | bytes 1048576 | tf_op jit(solution)/shard_map/pallas_call | solution.py:473
  (2 shorter events, 0.0 us)
Async XLA Ops:
  0.0 2.3 %collective-permute-start = (f32[2,2,4,1024]{3,2,1,0:T(4,128)}, f32[2,2,4,1024]{3,2,1,0:T(4,128)S(1)}, u32[]{:S(2)}, u32[]{:S(2)}) collective-permute-start(f32[2,2,4,1024]{3,2,1,0:T(4,128)} %refs_0_.1), channel_id=1, source_target_pairs={{0,1},{1,0},{2,3},{3,2},{4,5},{5,4},{6,7},{7,6},{8,9},{9,8},{10,11... | collective-permute-start | bytes 196616 | tf_op jit(solution)/shard_map/ppermute | solution.py:406
  0.5 0.7 %copy-start.1 = (s32[1024]{0:T(1024)S(1)}, s32[1024]{0:T(1024)}, u32[]{:S(2)}) copy-start(s32[1024]{0:T(1024)} %param.10) | copy-start | bytes 12292
  0.5 18.3 %collective-permute-start.1 = (bf16[4096,256]{1,0:T(8,128)(2,1)}, bf16[4096,256]{1,0:T(8,128)(2,1)}, u32[]{:S(2)}, u32[]{:S(2)}) collective-permute-start(bf16[4096,256]{1,0:T(8,128)(2,1)} %bitcast.11), channel_id=1, source_target_pairs={{0,1},{1,0},{2,3},{3,2},{4,5},{5,4},{6,7},{7,6},{8,9},{9,8},{10,11... | collective-permute-start | bytes 6291464 | tf_op jit(solution)/shard_map/ppermute | solution.py:407
  1.2 0.9 %copy-start.2 = (s32[32]{0:T(128)S(1)}, s32[32]{0:T(128)}, u32[]{:S(2)}) copy-start(s32[32]{0:T(128)} %param.11) | copy-start | bytes 388
  1.2 1.1 %copy-start = (f32[2,2,4,1024]{3,2,1,0:T(4,128)S(1)}, f32[2,2,4,1024]{3,2,1,0:T(4,128)}, u32[]{:S(2)}) copy-start(f32[2,2,4,1024]{3,2,1,0:T(4,128)} %refs_0_.1) | copy-start | bytes 196612
  1.2 1.1 %copy-start.3 = (f32[32]{0:T(128)S(1)}, f32[32]{0:T(128)}, u32[]{:S(2)}) copy-start(f32[32]{0:T(128)} %param.9) | copy-start | bytes 388
  1.2 9.4 %copy-start.5 = (f32[2,2,256]{2,1,0:T(2,128)S(1)}, f32[2,2,256]{2,1,0:T(2,128)}, u32[]{:S(2)}) copy-start(f32[2,2,256]{2,1,0:T(2,128)} %own_love_ref.1) | copy-start | bytes 12292
  1.6 17.1 %copy-start.4 = (bf16[128,256,32]{1,2,0:T(8,128)(2,1)S(1)}, bf16[128,256,32]{1,2,0:T(8,128)(2,1)}, u32[]{:S(2)}) copy-start(bf16[128,256,32]{1,2,0:T(8,128)(2,1)} %param.7) | copy-start | bytes 6291460
  3.6 15.2 %all-to-all-start = ((f32[32,8,128]{2,1,0:T(8,128)}), f32[32,8,128]{2,1,0:T(8,128)S(1)}, u32[]{:S(2)}, u32[]{:S(2)}) async-start(f32[32,8,128]{2,1,0:T(8,128)} %shard_map.68), calls=%async_computation | async-start | bytes 262144 | tf_op jit(solution)/shard_map/all_to_all | solution.py:453
  10.6 8.2 %collective-permute-start.2 = (f32[2,2,256]{2,1,0:T(2,128)S(1)}, f32[2,2,256]{2,1,0:T(2,128)S(1)}, u32[]{:S(2)}, u32[]{:S(2)}) collective-permute-start(f32[2,2,256]{2,1,0:T(2,128)S(1)} %copy-done.5), channel_id=1, source_target_pairs={{0,1},{1,0},{2,3},{3,2},{4,5},{5,4},{6,7},{7,6},{8,9},{9,8},{10,11... | collective-permute-start | bytes 12296 | tf_op jit(solution)/shard_map/ppermute | solution.py:408
where the time goes:
time: 33.5 us; the launch traced here: 33.3 us
  blocking collectives  9.97 us (30%)
  waiting for transfers between devices  7.88 us (24%)
  starting transfers between devices  7.82 us (23%)
  Pallas kernels  6.82 us (20%)
  local copies, waits for them, and re-layouts  0.64 us (2%)
    all_to_all x1, blocking collectives, per_device_kernels(): lax.all_to_all(values, everyone, split_axis=0, concat_axis=0, tiled=True)  9.97 us
    all_to_all x1, waiting for transfers between devices, per_device_kernels(): lax.all_to_all(sums, everyone, split_axis=0, concat_axis=0, tiled=True)  7.88 us
    all_to_all x1, starting transfers between devices, per_device_kernels(): lax.all_to_all(sums, everyone, split_axis=0, concat_axis=0, tiled=True)  6.95 us
    pallas_call x1, Pallas kernels, per_device_kernels(): kernel(spectral, jax.ShapeDtypeStruct((devices, 4 * cycles, per_owner), j...  3.18 us
    pallas_call x1, Pallas kernels, per_device_kernels(): kernel(synthesise_grid, jax.ShapeDtypeStruct(loads.shape, jnp.float32), [...  1.3 us
    pallas_call x1, Pallas kernels, per_device_kernels(): kernel(functools.partial(analyse_grid, total), jax.ShapeDtypeStruct((devi...  1.29 us
  transfers between devices with their start and end apart: 4, of which 1 were waited for; matrix products, arithmetic and copies ran while one was open for 0% of the time, Pallas kernels for 7%

commit v1 on v0

--- a/solution.py
+++ b/solution.py
@@ -68,17 +68,25 @@
                 at = ((q * blocks + a) * 2 + f) * step
                 points_ref[at : at + step] = jnp.concatenate([north + south, north - south], axis=0)
     high, low = split(points_ref[...])
-    mid_ref[...] = dot(jnp.concatenate([high, low, high], axis=1), right_ref[...])
-
-    sums = [[jnp.zeros((step, width), jnp.float32) for _ in range(2)] for _ in range(2)]
-    for a in range(count):
-        ca, sa = turn_ref[0, a : a + 1], turn_ref[1, a : a + 1]
-        for f in range(2):
-            at = (a * 2 + f) * step
-            tc = mid_ref[at : at + step, :width]
-            ts = mid_ref[at : at + step, width:]
-            sums[f][0] = sums[f][0] + (ca * tc - sa * ts)
-            sums[f][1] = sums[f][1] - (sa * tc + ca * ts)
+    left = jnp.concatenate([high, low, high], axis=1)
+    tiles = [slice(t * LANES, (t + 1) * LANES) for t in range(width // LANES)]
+    for t, lanes in enumerate(tiles):
+        sine = slice(width + t * LANES, width + (t + 1) * LANES)
+        right = jnp.concatenate([right_ref[:, lanes], right_ref[:, sine]], axis=1)
+        mid_ref[:, 2 * t * LANES : 2 * (t + 1) * LANES] = dot(left, right)
+
+    sums = []
+    for t, lanes in enumerate(tiles):
+        parts_of = [[jnp.zeros((step, LANES), jnp.float32) for _ in range(2)] for _ in range(2)]
+        for a in range(count):
+            ca, sa = turn_ref[0, a : a + 1, lanes], turn_ref[1, a : a + 1, lanes]
+            for f in range(2):
+                at = (a * 2 + f) * step
+                tc = mid_ref[at : at + step, 2 * t * LANES : (2 * t + 1) * LANES]
+                ts = mid_ref[at : at + step, (2 * t + 1) * LANES : 2 * (t + 1) * LANES]
+                parts_of[f][0] = parts_of[f][0] + (ca * tc - sa * ts)
+                parts_of[f][1] = parts_of[f][1] - (sa * tc + ca * ts)
+        sums.append(parts_of)
 
     slot = iota((1, LANES), 1) // quarter
     northern = cycle_ref.shape[1]
@@ -92,7 +100,7 @@
             t, i = (2 * owner + side) // pieces, (2 * owner + side) % pieces
             block = None
             for e in range(4):
-                piece = sums[e // 2][e % 2][:, t * LANES : (t + 1) * LANES]
+                piece = sums[t][e // 2][e % 2]
                 move = (e - i) * quarter % LANES
                 piece = pltpu.roll(piece, move, 1) if move else piece
                 block = piece if block is None else jnp.where(slot == e, piece, block)
@@ -209,7 +217,7 @@
             if k % 2 == 1:
                 rows = slice((k - 1) * ROWS, (k + 1) * ROWS)
                 for c in range(2):
-                    at = (c * owners + b) * per_owner
+                    at = (b * 2 + c) * per_owner
                     both = jnp.concatenate([kept[k - 1][c], kept[k][c]], axis=0)
                     basis_ref[rows, at : at + per_owner] = both.astype(basis_ref.dtype)
 
@@ -303,17 +311,17 @@
 
     steps = [(n, d) for n in range(groups) for d in range(2)]
     left, analysed, partial = None, {}, {}
-    for i in range(len(steps) + 2):
+    for i in range(len(steps) + 3):
         if i < len(steps):
             n, d = steps[i]
             left = spread(n) if d == 0 else left
             analysed[i] = dot(left, table(n, d))
-        if 1 <= i <= len(steps):
-            n, d = steps[i - 1]
-            value = respond(n, d, analysed.pop(i - 1))
+        if 2 <= i < len(steps) + 2:
+            n, d = steps[i - 2]
+            value = respond(n, d, analysed.pop(i - 2))
             partial[n] = value if d == 0 else partial[n] + value
-        if i >= 5 and i % 4 == 1:
-            n = (i - 5) // 2
+        if i >= 6 and i % 4 == 2:
+            n = (i - 6) // 2
             keep_pair(n, [partial.pop(n), partial.pop(n + 1)])
 
     total = dot_nt(put_ref[0], kept_ref[0]) + dot_nt(put_ref[1], kept_ref[1])
@@ -330,7 +338,6 @@
     lon_count = values_ref.shape[0] // owners
     rows = values_ref.shape[1]
     cycles = out_ref.shape[2]
-    count = owners * per_owner
     height = blocks * rows
     first_lanes = iota((1, LANES), 1) < per_owner // 2
     for b in range(owners):
@@ -342,15 +349,19 @@
             halves.append(value)
         re = jnp.where(first_lanes, halves[0], pltpu.roll(halves[1], per_owner // 2, 1))
         im = jnp.where(first_lanes, pltpu.roll(halves[0], per_owner // 2, 1), halves[1])
-        at = b * per_owner
+        at = 2 * b * per_owner
         for a in range(blocks):
             ca, sa = turn_ref[0, b, a : a + 1], turn_ref[1, b, a : a + 1]
             for c, term in ((0, ca * re - sa * im), (1, -(sa * re + ca * im))):
                 high, low = split(term)
-                lanes = slice(c * count + at, c * count + at + per_owner)
+                lanes = slice(at + c * per_owner, at + (c + 1) * per_owner)
                 left_ref[a * rows : (a + 1) * rows, lanes] = high
                 left_ref[height + a * rows : height + (a + 1) * rows, lanes] = low
-    grid = dot_nt(left_ref[...], basis_ref[...])
+    grid = None
+    for b in range(owners):
+        lanes = slice(2 * b * per_owner, 2 * (b + 1) * per_owner)
+        term = dot_nt(left_ref[:, lanes], basis_ref[:, lanes])
+        grid = term if grid is None else grid + term
     grid = grid[:height] + grid[height:]
     for a in range(blocks):
         for g in range(2):

time: 33.5 us -> 33.3 us (level)
  no operation moved by 1% of the time
where the time goes in v1:
time: 33.3 us; the launch traced here: 33.1 us
  blocking collectives  9.97 us (30%)
  waiting for transfers between devices  7.88 us (24%)
  starting transfers between devices  7.82 us (23%)
  Pallas kernels  6.63 us (20%)
  local copies, waits for them, and re-layouts  0.64 us (2%)
    all_to_all x1, blocking collectives, per_device_kernels(): lax.all_to_all(values, everyone, split_axis=0, concat_axis=0, tiled=True)  9.97 us
    all_to_all x1, waiting for transfers between devices, per_device_kernels(): lax.all_to_all(sums, everyone, split_axis=0, concat_axis=0, tiled=True)  7.88 us
    all_to_all x1, starting transfers between devices, per_device_kernels(): lax.all_to_all(sums, everyone, split_axis=0, concat_axis=0, tiled=True)  6.95 us
    pallas_call x1, Pallas kernels, per_device_kernels(): kernel(spectral, jax.ShapeDtypeStruct((devices, 4 * cycles, per_owner), j...  3.11 us
    pallas_call x1, Pallas kernels, per_device_kernels(): kernel(synthesise_grid, jax.ShapeDtypeStruct(loads.shape, jnp.float32), [...  1.3 us
    pallas_call x1, Pallas kernels, per_device_kernels(): kernel(functools.partial(analyse_grid, total), jax.ShapeDtypeStruct((devi...  1.19 us
  transfers between devices with their start and end apart: 4, of which 1 were waited for; matrix products, arithmetic and copies ran while one was open for 0% of the time, Pallas kernels for 7%

profile of v1, /device:TPU:0, one launch (start us, length us, event | category | flops | bytes accessed | tf_op | source)
XLA Modules:
  0.0 33.1 jit_solution(12006560842646340915)
XLA Ops:
  0.0 0.5 %collective-permute-start = (f32[2,2,4,1024]{3,2,1,0:T(4,128)}, f32[2,2,4,1024]{3,2,1,0:T(4,128)S(1)}, u32[]{:S(2)}, u32[]{:S(2)}) collective-permute-start(f32[2,2,4,1024]{3,2,1,0:T(4,128)} %refs_0_.1), channel_id=1, source_target_pairs={{0,1},{1,0},{2,3},{3,2},{4,5},{5,4},{6,7},{7,6},{8,9},{9,8},{10,11... | collective-permute-start | bytes 196616 | tf_op jit(solution)/shard_map/ppermute | solution.py:417
  0.5 0.0 copy-start.1
  0.5 0.1 collective-permute-start.1
  0.6 0.6 %copy-done.1 = s32[1024]{0:T(1024)S(1)} copy-done((s32[1024]{0:T(1024)S(1)}, s32[1024]{0:T(1024)}, u32[]{:S(2)}) %copy-start.1) | copy-done | bytes 4120
  1.2 0.0 copy-start.2
  1.2 0.0 copy-start
  1.2 0.0 copy-start.3
  1.2 0.0 copy-start.5
  1.2 0.5 %shard_map.65 = (bf16[384,1024]{1,0:T(8,128)(2,1)S(1)}, f32[2,16,512]{2,1,0:T(8,128)S(1)}) custom-call(s32[8,128]{1,0:T(8,128)S(1)} %bitcast.6, f32[8,128]{1,0:T(8,128)S(1)} %shard_map.64.after_ref), custom_call_target="tpu_custom_call" | custom-call | flops 17179869184 | bytes 1048576 | tf_op jit(solution)/shard_map/pallas_call | solution.py:423
  1.6 0.0 copy-start.4
  1.7 0.4 %shard_map.66 = (s32[128,128]{1,0:T(8,128)S(1)}, f32[2,8,8,128]{3,2,1,0:T(8,128)S(1)}, bf16[128,2048]{1,0:T(8,128)(2,1)S(1)}) custom-call(s32[8,128]{1,0:T(8,128)S(1)} %bitcast.7, f32[2,16,512]{2,1,0:T(8,128)S(1)} %get-tuple-element.12.after_ref.turn_ref), custom_call_target="tpu_custom_call" | custom-call | flops 1048576 | bytes 1048576 | tf_op jit(solution)/shard_map/pallas_call | solution.py:433
  2.1 0.0 copy-done.2
  2.1 0.2 shard_map.67
  2.3 0.0 collective-permute-done.refs_1_
  2.3 0.0 copy-done
  2.3 0.0 copy-done.3
  2.3 1.2 %shard_map.68 = f32[32,8,128]{2,1,0:T(8,128)} custom-call(bf16[256,128]{1,0:T(8,128)(2,1)S(1)} %get-tuple-element.16.after_ref.pick_ref, bf16[384,1024]{1,0:T(8,128)(2,1)S(1)} %get-tuple-element.18.right_ref, f32[2,16,512]{2,1,0:T(8,128)S(1)} %get-tuple-element.12.after_ref.turn_ref, f32[1,32]{1,0:T(1,128)S(1)} %bitcast.10, s32[1,32]{1,0:T(1,128)S(1)} %bitcast.9, ...), custom_call_target="tpu_custom_call" | custom-call | flops 16777216 | bytes 1048576 | tf_op jit(solution)/shard_map/pallas_call | solution.py:454
  3.5 6.9 %all-to-all-start = ((f32[32,8,128]{2,1,0:T(8,128)}), f32[32,8,128]{2,1,0:T(8,128)S(1)}, u32[]{:S(2)}, u32[]{:S(2)}) async-start(f32[32,8,128]{2,1,0:T(8,128)} %shard_map.68), calls=%async_computation | async-start | bytes 262144 | tf_op jit(solution)/shard_map/all_to_all | solution.py:464
  10.4 0.0 copy-done.5
  10.4 0.3 collective-permute-start.2
  10.8 7.9 %all-to-all-done.parts_ref = f32[32,8,128]{2,1,0:T(8,128)S(1)} async-done(((f32[32,8,128]{2,1,0:T(8,128)}), f32[32,8,128]{2,1,0:T(8,128)S(1)}, u32[]{:S(2)}, u32[]{:S(2)}) %all-to-all-start) | async-done | bytes 131104 | tf_op jit(solution)/shard_map/all_to_all | solution.py:464
  18.6 0.0 collective-permute-done.2.other_love_ref
  18.7 0.0 collective-permute-done.1.other_table_ref
  18.7 0.0 copy-done.4
  18.7 3.1 %shard_map.70 = bf16[32,16,128]{2,1,0:T(8,128)(2,1)S(1)} custom-call(bf16[256,128]{1,0:T(8,128)(2,1)S(1)} %get-tuple-element.16.after_ref.pick_ref, bf16[2,128,256]{2,1,0:T(8,128)(2,1)S(1)} %get-tuple-element.17.put_ref, s32[128,128]{1,0:T(8,128)S(1)} %get-tuple-element.15.after_ref.rows_ref, bf16[2,8,8,128]{3,2,1,0:T(8,128)(2,1)S(1)} %shard_map.69.folded_ref, ...), custom_call_target="tpu_custom_call" | custom-call | flops 2147483648 | bytes 1048576 | tf_op jit(solution)/shard_map/pallas_call | solution.py:472
  21.8 10.0 %all_to_all.10.values_ref = bf16[32,16,128]{2,1,0:T(8,128)(2,1)S(1)} all-to-all(bf16[32,16,128]{2,1,0:T(8,128)(2,1)S(1)} %shard_map.70), channel_id=1, replica_groups=mesh['band'=8,'lon'=4] {'band','lon'}, dimensions={0} | all-to-all | bytes 262144 | tf_op jit(solution)/shard_map/all_to_all | solution.py:482
  31.8 1.3 %shard_map.71 = f32[2,2,4,1024]{3,2,1,0:T(4,128)} custom-call(f32[2,8,8,128]{3,2,1,0:T(8,128)S(1)} %get-tuple-element.13.turn_ref, bf16[128,2048]{1,0:T(8,128)(2,1)S(1)} %get-tuple-element.14.basis_ref, bf16[32,16,128]{2,1,0:T(8,128)(2,1)S(1)} %all_to_all.10.values_ref), custom_call_target="tpu_custom_call" | custom-call | flops 2147483648 | bytes 1048576 | tf_op jit(solution)/shard_map/pallas_call | solution.py:484
  (2 shorter events, 0.0 us)
Async XLA Ops:
  0.0 2.3 %collective-permute-start = (f32[2,2,4,1024]{3,2,1,0:T(4,128)}, f32[2,2,4,1024]{3,2,1,0:T(4,128)S(1)}, u32[]{:S(2)}, u32[]{:S(2)}) collective-permute-start(f32[2,2,4,1024]{3,2,1,0:T(4,128)} %refs_0_.1), channel_id=1, source_target_pairs={{0,1},{1,0},{2,3},{3,2},{4,5},{5,4},{6,7},{7,6},{8,9},{9,8},{10,11... | collective-permute-start | bytes 196616 | tf_op jit(solution)/shard_map/ppermute | solution.py:417
  0.5 0.7 %copy-start.1 = (s32[1024]{0:T(1024)S(1)}, s32[1024]{0:T(1024)}, u32[]{:S(2)}) copy-start(s32[1024]{0:T(1024)} %param.10) | copy-start | bytes 12292
  0.5 18.2 %collective-permute-start.1 = (bf16[4096,256]{1,0:T(8,128)(2,1)}, bf16[4096,256]{1,0:T(8,128)(2,1)}, u32[]{:S(2)}, u32[]{:S(2)}) collective-permute-start(bf16[4096,256]{1,0:T(8,128)(2,1)} %bitcast.11), channel_id=1, source_target_pairs={{0,1},{1,0},{2,3},{3,2},{4,5},{5,4},{6,7},{7,6},{8,9},{9,8},{10,11... | collective-permute-start | bytes 6291464 | tf_op jit(solution)/shard_map/ppermute | solution.py:418
  1.2 0.9 %copy-start.2 = (s32[32]{0:T(128)S(1)}, s32[32]{0:T(128)}, u32[]{:S(2)}) copy-start(s32[32]{0:T(128)} %param.11) | copy-start | bytes 388
  1.2 1.1 %copy-start = (f32[2,2,4,1024]{3,2,1,0:T(4,128)S(1)}, f32[2,2,4,1024]{3,2,1,0:T(4,128)}, u32[]{:S(2)}) copy-start(f32[2,2,4,1024]{3,2,1,0:T(4,128)} %refs_0_.1) | copy-start | bytes 196612
  1.2 1.1 %copy-start.3 = (f32[32]{0:T(128)S(1)}, f32[32]{0:T(128)}, u32[]{:S(2)}) copy-start(f32[32]{0:T(128)} %param.9) | copy-start | bytes 388
  1.2 9.2 %copy-start.5 = (f32[2,2,256]{2,1,0:T(2,128)S(1)}, f32[2,2,256]{2,1,0:T(2,128)}, u32[]{:S(2)}) copy-start(f32[2,2,256]{2,1,0:T(2,128)} %own_love_ref.1) | copy-start | bytes 12292
  1.6 17.0 %copy-start.4 = (bf16[128,256,32]{1,2,0:T(8,128)(2,1)S(1)}, bf16[128,256,32]{1,2,0:T(8,128)(2,1)}, u32[]{:S(2)}) copy-start(bf16[128,256,32]{1,2,0:T(8,128)(2,1)} %param.7) | copy-start | bytes 6291460
  3.5 15.2 %all-to-all-start = ((f32[32,8,128]{2,1,0:T(8,128)}), f32[32,8,128]{2,1,0:T(8,128)S(1)}, u32[]{:S(2)}, u32[]{:S(2)}) async-start(f32[32,8,128]{2,1,0:T(8,128)} %shard_map.68), calls=%async_computation | async-start | bytes 262144 | tf_op jit(solution)/shard_map/all_to_all | solution.py:464
  10.4 8.2 %collective-permute-start.2 = (f32[2,2,256]{2,1,0:T(2,128)S(1)}, f32[2,2,256]{2,1,0:T(2,128)S(1)}, u32[]{:S(2)}, u32[]{:S(2)}) collective-permute-start(f32[2,2,256]{2,1,0:T(2,128)S(1)} %copy-done.5), channel_id=1, source_target_pairs={{0,1},{1,0},{2,3},{3,2},{4,5},{5,4},{6,7},{7,6},{8,9},{9,8},{10,11... | collective-permute-start | bytes 12296 | tf_op jit(solution)/shard_map/ppermute | solution.py:419

commit v2 on v1

--- a/solution.py
+++ b/solution.py
@@ -130,6 +130,14 @@
     out_ref[...] = jnp.zeros_like(out_ref)
 
 
+def coarse_turns(orders, total):
+    half = LANES // ROWS // 2
+    c, s = turn((iota((half, orders.shape[1]), 0) * ROWS * orders) & (total - 1), total)
+    last, one = slice(half - 1, half), slice(1, 2)
+    rc, rs = c[last] * c[one] - s[last] * s[one], s[last] * c[one] + c[last] * s[one]
+    return jnp.concatenate([c, c * rc - s * rs], axis=0), jnp.concatenate([s, s * rc + c * rs], axis=0)
+
+
 def forward_tables(blocks, total, orders_ref, after_ref, right_ref, first_ref):
     del after_ref
     owners, per_owner = orders_ref.shape
@@ -145,7 +153,7 @@
     )
     width = orders.shape[1]
     fine = turn(iota((ROWS, width), 0) * orders, total)
-    coarse = turn((iota((LANES // ROWS, width), 0) * ROWS * orders) & (total - 1), total)
+    coarse = coarse_turns(orders, total)
     kept = []
     for k, pair in enumerate(products(fine, coarse)):
         kept.append([split(table) for table in pair])
@@ -210,7 +218,7 @@
         for c, table in enumerate(turn((step * LANES * order) & (total - 1), total)):
             turn_ref[c, b] = table * factor
         fine = turn(iota((ROWS, per_owner), 0) * order, total)
-        coarse = turn((iota((LANES // ROWS, per_owner), 0) * ROWS * order) & (total - 1), total)
+        coarse = coarse_turns(order, total)
         kept = []
         for k, pair in enumerate(products(fine, coarse)):
             kept.append(pair)

time: 33.3 us -> 33.3 us (level)
  no operation moved by 1% of the time
where the time goes in v2:
time: 33.3 us; the launch traced here: 33 us
  blocking collectives  9.96 us (30%)
  waiting for transfers between devices  7.88 us (24%)
  starting transfers between devices  7.82 us (23%)
  Pallas kernels  6.6 us (20%)
  local copies, waits for them, and re-layouts  0.64 us (2%)
    all_to_all x1, blocking collectives, per_device_kernels(): lax.all_to_all(values, everyone, split_axis=0, concat_axis=0, tiled=True)  9.96 us
    all_to_all x1, waiting for transfers between devices, per_device_kernels(): lax.all_to_all(sums, everyone, split_axis=0, concat_axis=0, tiled=True)  7.88 us
    all_to_all x1, starting transfers between devices, per_device_kernels(): lax.all_to_all(sums, everyone, split_axis=0, concat_axis=0, tiled=True)  6.95 us
    pallas_call x1, Pallas kernels, per_device_kernels(): kernel(spectral, jax.ShapeDtypeStruct((devices, 4 * cycles, per_owner), j...  3.11 us
    pallas_call x1, Pallas kernels, per_device_kernels(): kernel(synthesise_grid, jax.ShapeDtypeStruct(loads.shape, jnp.float32), [...  1.3 us
    pallas_call x1, Pallas kernels, per_device_kernels(): kernel(functools.partial(analyse_grid, total), jax.ShapeDtypeStruct((devi...  1.19 us
  transfers between devices with their start and end apart: 4, of which 1 were waited for; matrix products, arithmetic and copies ran while one was open for 0% of the time, Pallas kernels for 7%

profile of v2, /device:TPU:0, one launch (start us, length us, event | category | flops | bytes accessed | tf_op | source)
XLA Modules:
  0.0 33.0 jit_solution(14639027740186670182)
XLA Ops:
  0.0 0.5 %collective-permute-start = (f32[2,2,4,1024]{3,2,1,0:T(4,128)}, f32[2,2,4,1024]{3,2,1,0:T(4,128)S(1)}, u32[]{:S(2)}, u32[]{:S(2)}) collective-permute-start(f32[2,2,4,1024]{3,2,1,0:T(4,128)} %refs_0_.1), channel_id=1, source_target_pairs={{0,1},{1,0},{2,3},{3,2},{4,5},{5,4},{6,7},{7,6},{8,9},{9,8},{10,11... | collective-permute-start | bytes 196616 | tf_op jit(solution)/shard_map/ppermute | solution.py:425
  0.5 0.0 copy-start.1
  0.5 0.1 collective-permute-start.1
  0.6 0.6 %copy-done.1 = s32[1024]{0:T(1024)S(1)} copy-done((s32[1024]{0:T(1024)S(1)}, s32[1024]{0:T(1024)}, u32[]{:S(2)}) %copy-start.1) | copy-done | bytes 4120
  1.2 0.0 copy-start.2
  1.2 0.0 copy-start
  1.2 0.0 copy-start.3
  1.2 0.0 copy-start.5
  1.2 0.4 %shard_map.65 = (bf16[384,1024]{1,0:T(8,128)(2,1)S(1)}, f32[2,16,512]{2,1,0:T(8,128)S(1)}) custom-call(s32[8,128]{1,0:T(8,128)S(1)} %bitcast.6, f32[8,128]{1,0:T(8,128)S(1)} %shard_map.64.after_ref), custom_call_target="tpu_custom_call" | custom-call | flops 17179869184 | bytes 1048576 | tf_op jit(solution)/shard_map/pallas_call | solution.py:431
  1.6 0.0 copy-start.4
  1.6 0.4 %shard_map.66 = (s32[128,128]{1,0:T(8,128)S(1)}, f32[2,8,8,128]{3,2,1,0:T(8,128)S(1)}, bf16[128,2048]{1,0:T(8,128)(2,1)S(1)}) custom-call(s32[8,128]{1,0:T(8,128)S(1)} %bitcast.7, f32[2,16,512]{2,1,0:T(8,128)S(1)} %get-tuple-element.12.after_ref.turn_ref), custom_call_target="tpu_custom_call" | custom-call | flops 1048576 | bytes 1048576 | tf_op jit(solution)/shard_map/pallas_call | solution.py:441
  2.0 0.0 copy-done.2
  2.0 0.2 shard_map.67
  2.2 0.0 collective-permute-done.refs_1_
  2.2 0.0 copy-done
  2.2 0.0 copy-done.3
  2.3 1.2 %shard_map.68 = f32[32,8,128]{2,1,0:T(8,128)} custom-call(bf16[256,128]{1,0:T(8,128)(2,1)S(1)} %get-tuple-element.16.after_ref.pick_ref, bf16[384,1024]{1,0:T(8,128)(2,1)S(1)} %get-tuple-element.18.right_ref, f32[2,16,512]{2,1,0:T(8,128)S(1)} %get-tuple-element.12.after_ref.turn_ref, f32[1,32]{1,0:T(1,128)S(1)} %bitcast.10, s32[1,32]{1,0:T(1,128)S(1)} %bitcast.9, ...), custom_call_target="tpu_custom_call" | custom-call | flops 16777216 | bytes 1048576 | tf_op jit(solution)/shard_map/pallas_call | solution.py:462
  3.4 6.9 %all-to-all-start = ((f32[32,8,128]{2,1,0:T(8,128)}), f32[32,8,128]{2,1,0:T(8,128)S(1)}, u32[]{:S(2)}, u32[]{:S(2)}) async-start(f32[32,8,128]{2,1,0:T(8,128)} %shard_map.68), calls=%async_computation | async-start | bytes 262144 | tf_op jit(solution)/shard_map/all_to_all | solution.py:472
  10.4 0.0 copy-done.5
  10.4 0.3 collective-permute-start.2
  10.7 7.9 %all-to-all-done.parts_ref = f32[32,8,128]{2,1,0:T(8,128)S(1)} async-done(((f32[32,8,128]{2,1,0:T(8,128)}), f32[32,8,128]{2,1,0:T(8,128)S(1)}, u32[]{:S(2)}, u32[]{:S(2)}) %all-to-all-start) | async-done | bytes 131104 | tf_op jit(solution)/shard_map/all_to_all | solution.py:472
  18.6 0.0 collective-permute-done.2.other_love_ref
  18.6 0.0 collective-permute-done.1.other_table_ref
  18.6 0.0 copy-done.4
  18.6 3.1 %shard_map.70 = bf16[32,16,128]{2,1,0:T(8,128)(2,1)S(1)} custom-call(bf16[256,128]{1,0:T(8,128)(2,1)S(1)} %get-tuple-element.16.after_ref.pick_ref, bf16[2,128,256]{2,1,0:T(8,128)(2,1)S(1)} %get-tuple-element.17.put_ref, s32[128,128]{1,0:T(8,128)S(1)} %get-tuple-element.15.after_ref.rows_ref, bf16[2,8,8,128]{3,2,1,0:T(8,128)(2,1)S(1)} %shard_map.69.folded_ref, ...), custom_call_target="tpu_custom_call" | custom-call | flops 2147483648 | bytes 1048576 | tf_op jit(solution)/shard_map/pallas_call | solution.py:480
  21.8 10.0 %all_to_all.10.values_ref = bf16[32,16,128]{2,1,0:T(8,128)(2,1)S(1)} all-to-all(bf16[32,16,128]{2,1,0:T(8,128)(2,1)S(1)} %shard_map.70), channel_id=1, replica_groups=mesh['band'=8,'lon'=4] {'band','lon'}, dimensions={0} | all-to-all | bytes 262144 | tf_op jit(solution)/shard_map/all_to_all | solution.py:490
  31.7 1.3 %shard_map.71 = f32[2,2,4,1024]{3,2,1,0:T(4,128)} custom-call(f32[2,8,8,128]{3,2,1,0:T(8,128)S(1)} %get-tuple-element.13.turn_ref, bf16[128,2048]{1,0:T(8,128)(2,1)S(1)} %get-tuple-element.14.basis_ref, bf16[32,16,128]{2,1,0:T(8,128)(2,1)S(1)} %all_to_all.10.values_ref), custom_call_target="tpu_custom_call" | custom-call | flops 2147483648 | bytes 1048576 | tf_op jit(solution)/shard_map/pallas_call | solution.py:492
  (2 shorter events, 0.0 us)
Async XLA Ops:
  0.0 2.2 %collective-permute-start = (f32[2,2,4,1024]{3,2,1,0:T(4,128)}, f32[2,2,4,1024]{3,2,1,0:T(4,128)S(1)}, u32[]{:S(2)}, u32[]{:S(2)}) collective-permute-start(f32[2,2,4,1024]{3,2,1,0:T(4,128)} %refs_0_.1), channel_id=1, source_target_pairs={{0,1},{1,0},{2,3},{3,2},{4,5},{5,4},{6,7},{7,6},{8,9},{9,8},{10,11... | collective-permute-start | bytes 196616 | tf_op jit(solution)/shard_map/ppermute | solution.py:425
  0.5 0.7 %copy-start.1 = (s32[1024]{0:T(1024)S(1)}, s32[1024]{0:T(1024)}, u32[]{:S(2)}) copy-start(s32[1024]{0:T(1024)} %param.10) | copy-start | bytes 12292
  0.5 18.1 %collective-permute-start.1 = (bf16[4096,256]{1,0:T(8,128)(2,1)}, bf16[4096,256]{1,0:T(8,128)(2,1)}, u32[]{:S(2)}, u32[]{:S(2)}) collective-permute-start(bf16[4096,256]{1,0:T(8,128)(2,1)} %bitcast.11), channel_id=1, source_target_pairs={{0,1},{1,0},{2,3},{3,2},{4,5},{5,4},{6,7},{7,6},{8,9},{9,8},{10,11... | collective-permute-start | bytes 6291464 | tf_op jit(solution)/shard_map/ppermute | solution.py:426
  1.2 0.9 %copy-start.2 = (s32[32]{0:T(128)S(1)}, s32[32]{0:T(128)}, u32[]{:S(2)}) copy-start(s32[32]{0:T(128)} %param.11) | copy-start | bytes 388
  1.2 1.0 %copy-start = (f32[2,2,4,1024]{3,2,1,0:T(4,128)S(1)}, f32[2,2,4,1024]{3,2,1,0:T(4,128)}, u32[]{:S(2)}) copy-start(f32[2,2,4,1024]{3,2,1,0:T(4,128)} %refs_0_.1) | copy-start | bytes 196612
  1.2 1.1 %copy-start.3 = (f32[32]{0:T(128)S(1)}, f32[32]{0:T(128)}, u32[]{:S(2)}) copy-start(f32[32]{0:T(128)} %param.9) | copy-start | bytes 388
  1.2 9.2 %copy-start.5 = (f32[2,2,256]{2,1,0:T(2,128)S(1)}, f32[2,2,256]{2,1,0:T(2,128)}, u32[]{:S(2)}) copy-start(f32[2,2,256]{2,1,0:T(2,128)} %own_love_ref.1) | copy-start | bytes 12292
  1.6 17.0 %copy-start.4 = (bf16[128,256,32]{1,2,0:T(8,128)(2,1)S(1)}, bf16[128,256,32]{1,2,0:T(8,128)(2,1)}, u32[]{:S(2)}) copy-start(bf16[128,256,32]{1,2,0:T(8,128)(2,1)} %param.7) | copy-start | bytes 6291460
  3.4 15.2 %all-to-all-start = ((f32[32,8,128]{2,1,0:T(8,128)}), f32[32,8,128]{2,1,0:T(8,128)S(1)}, u32[]{:S(2)}, u32[]{:S(2)}) async-start(f32[32,8,128]{2,1,0:T(8,128)} %shard_map.68), calls=%async_computation | async-start | bytes 262144 | tf_op jit(solution)/shard_map/all_to_all | solution.py:472
  10.4 8.2 %collective-permute-start.2 = (f32[2,2,256]{2,1,0:T(2,128)S(1)}, f32[2,2,256]{2,1,0:T(2,128)S(1)}, u32[]{:S(2)}, u32[]{:S(2)}) collective-permute-start(f32[2,2,256]{2,1,0:T(2,128)S(1)} %copy-done.5), channel_id=1, source_target_pairs={{0,1},{1,0},{2,3},{3,2},{4,5},{5,4},{6,7},{7,6},{8,9},{9,8},{10,11... | collective-permute-start | bytes 12296 | tf_op jit(solution)/shard_map/ppermute | solution.py:427
